TPU v7x, 256 devices: a whole 4x4x8 slice. The times are simulated.
256 devices in a mesh: front: 4 (over x), row: 8 (over z_hi, core), col: 8 (over y, z_lo).
Axes of the slice: x: 4, y: 4, z: 8 (z_hi: 4, z_lo: 2; z = z_hi * 2 + z_lo), core: 2. Of those that a mesh axis runs over, the one named last changes fastest.
Arguments:
- front: bfloat16 [4, 12288, 12288], P('front', 'row', 'col'), may hold values from -6 to 6
- panel: bfloat16 [4, 12288, 512], P('front', ('row', 'col')), may hold values from -8 to 8
- inverse: bfloat16 [4, 512, 512], P('front'), may hold values from -0.0046 to 0.056
- fill: int32 [4, 48], P('front'), may hold values 0 or 1
- block_map: int32 [4, 48], P('front'), may hold values from 0 to 47, as said below
- parent_front: bfloat16 [4, 6144, 12288], P('front', 'row', 'col'), may hold values from -6 to 6
Outputs:
- factor_rows: bfloat16 [4, 12288, 512], P('front', ('row', 'col'))
- parent: float32 [4, 6144, 12288], P('front', 'row', 'col')
Inputs may be any that keep to these rules, and one draw needn't show every extreme that they name: `block_map`: each front's map is a permutation of its blocks that keeps every aligned group of 6 blocks in place as a group.
All inputs are finite; a program needn't handle non-finite values. No bound on the sum of `fill` on one device may be relied on, other than what follows from the above.
Results may differ from a plain program's by a relative error of at most 0.0025.
Values may be sent and summed in bfloat16 or wider, within the bound.
A program may use at most 64 MiB of HBM per device.

v0:
```python
import jax
import jax.numpy as jnp
from jax import lax
from jax.sharding import PartitionSpec as P

BLK = 256


def from_partner(block, axis, distance):
    count = lax.axis_size(axis)
    route = []
    for low in range(count):
        high = low | 1 << distance
        if high != low and high < count:
            route += [(low, high), (high, low)]
    return lax.ppermute(block, axis, route)


def block_inverse(mapping, block_total):
    target = jnp.arange(block_total, dtype=jnp.int32)
    matches = (mapping[:, None] == target[None, :]).astype(jnp.int32)
    return jnp.sum(matches * target[:, None], axis=0)


def shards(front, panel, inverse, fill, block_map, parent_front):
    col_count = lax.axis_size("col")
    row_index = lax.axis_index("row")
    col_index = lax.axis_index("col")
    local_rows = panel.shape[1]
    tile_rows = front.shape[1]
    tile_cols = front.shape[2]
    block_total = fill.shape[1]
    first_row = (row_index * col_count + col_index) * local_rows
    positions = (first_row + jnp.arange(local_rows, dtype=jnp.int32)) // BLK
    blocks = jnp.arange(block_total, dtype=jnp.int32)
    row_fill = jnp.sum(
        (positions[:, None] == blocks[None, :]).astype(jnp.int32) * fill[0][None, :], axis=1
    )
    masked = panel[0] * row_fill[:, None].astype(jnp.bfloat16)
    factor = jnp.dot(masked, jnp.triu(inverse[0]), preferred_element_type=jnp.float32).astype(
        jnp.bfloat16
    )
    all_rows = lax.all_gather(factor, ("row", "col"), axis=0, tiled=True)
    row_side = lax.dynamic_slice_in_dim(all_rows, row_index * tile_rows, tile_rows, 0)
    col_side = lax.dynamic_slice_in_dim(all_rows, col_index * tile_cols, tile_cols, 0)
    contract = (((1,), (1,)), ((), ()))
    initial = front[0].astype(jnp.float32)
    row_blocks = tile_rows // BLK
    col_blocks = tile_cols // BLK
    update = lax.dot_general(row_side, col_side, contract, preferred_element_type=jnp.float32)
    schur = initial - update
    source = block_inverse(block_map[0], block_total)
    row_source = (
        lax.dynamic_slice_in_dim(source, row_index * row_blocks, row_blocks, 0)
        - row_index * row_blocks
    )
    col_source = (
        lax.dynamic_slice_in_dim(source, col_index * col_blocks, col_blocks, 0)
        - col_index * col_blocks
    )
    shaped = jnp.take(schur.reshape(row_blocks, BLK, tile_cols), row_source, axis=0)
    shaped = jnp.take(shaped.reshape(tile_rows, col_blocks, BLK), col_source, axis=1)
    contribution = shaped.reshape(tile_rows, tile_cols).astype(jnp.bfloat16)
    half_rows = tile_rows // 2
    parity = lax.axis_index("front") % 2
    kept_half = lax.dynamic_slice_in_dim(contribution, parity * half_rows, half_rows, 0)
    sent_half = lax.dynamic_slice_in_dim(contribution, (1 - parity) * half_rows, half_rows, 0)
    arrived = from_partner(sent_half, "front", 0)
    parent = (
        parent_front[0].astype(jnp.float32)
        + kept_half.astype(jnp.float32)
        + arrived.astype(jnp.float32)
    )
    return (factor[None], parent[None])


def solution(mesh):
    placed = (
        P("front", "row", "col"),
        P("front", ("row", "col"), None),
        P("front", None, None),
        P("front", None),
        P("front", None),
        P("front", "row", "col"),
    )
    return jax.shard_map(
        shards,
        mesh=mesh,
        in_specs=placed,
        out_specs=(P("front", ("row", "col"), None), P("front", "row", "col")),
        check_vma=False,
    )
```

profile of v0, /device:TPU:105, one launch (start us, length us, event | category | flops | bytes accessed | tf_op | source)
XLA Modules:
  0.0 335.8 jit_solution(6356897594682309380)
XLA Ops:
  7.2 0.0 all-gather.2.cloned.1.call-start
  7.2 0.7 select_reduce_fusion
  8.0 2.2 convolution_convert_fusion
  10.2 0.0 all-gather.2.cloned.1.call-update
  10.2 0.7 select_reduce_fusion.1
  11.0 0.1 compare_and_fusion.1
  11.1 0.1 broadcast_in_dim.52
  11.1 0.1 broadcast_in_dim.49
  11.3 204.7 %all-gather.2.cloned.1.call-done = bf16[12288,512]{1,0:T(8,128)(2,1)} async-done(((bf16[192,512]{1,0:T(8,128)(2,1)}), bf16[12288,512]{1,0:T(8,128)(2,1)}) %all-gather.2.cloned.1.call-update) | async-done | bytes 12582928 | tf_op jit(solution)/shard_map/all_gather | solution.py:43
  216.0 8.2 %convert_subtract_fusion = bf16[1536,1536]{1,0:T(8,128)(2,1)} fusion(bf16[1,1536,1536]{2,1,0:T(8,128)(2,1)} %param.6, bf16[12288,512]{1,0:T(8,128)(2,1)} %all-gather.2.cloned.1.call-done, s32[]{:T(128)S(6)} %select_n.68, s32[]{:T(128)S(6)} %select_n.67), kind=kOutput, calls=%fused_computation.2 | convolution fusion | flops 2422996992 | bytes 12582920 | tf_op jit(solution)/shard_map/dot_general | solution.py:50
  224.1 5.5 %gather_fusion = bf16[6,256,1536]{2,1,0:T(8,128)(2,1)} fusion(bf16[6,256,1536]{2,1,0:T(8,128)(2,1)} %bitcast.24, s32[1024]{0:T(1024)S(1)} %pad_clamp_fusion.1), kind=kCustom, calls=%fused_computation | custom fusion | bytes 9437208 | tf_op jit(solution)/shard_map/jit(_take)/gather | solution.py:61
  229.7 10.3 %gather.13 = bf16[1536,6,256]{2,1,0:T(8,128)(2,1)} reshape(bf16[6,256,1536]{2,1,0:T(8,128)(2,1)} %gather_fusion) | data formatting | bytes 9437184 | tf_op jit(solution)/shard_map/jit(_take)/gather | solution.py:61
  240.0 5.9 %copy_select_fusion = bf16[1536,6,256]{2,0,1:T(8,128)(2,1)} fusion(bf16[1536,6,256]{2,1,0:T(8,128)(2,1)} %gather.13, pred[1536]{0:T(1024)(128)(4,1)S(1)} %broadcast_in_dim.53), kind=kLoop, calls=%fused_computation.5 | loop fusion | flops 2359296 | bytes 9438720 | tf_op jit(solution)/shard_map/jit(_take)/select_n | solution.py:61
  245.8 5.5 %gather_fusion.1 = bf16[6,1536,256]{2,1,0:T(8,128)(2,1)} fusion(bf16[1536,6,256]{2,0,1:T(8,128)(2,1)} %copy_select_fusion, s32[1024]{0:T(1024)S(1)} %pad_clamp_fusion), kind=kCustom, calls=%fused_computation.1 | custom fusion | bytes 9437208 | tf_op jit(solution)/shard_map/jit(_take)/gather | solution.py:62
  251.3 6.6 %copy.14 = bf16[1536,6,256]{0,2,1:T(8,128)(2,1)} copy(bf16[1536,6,256]{2,0,1:T(8,128)(2,1)} %bitcast.23) | data formatting | bytes 9437184 | tf_op jit(solution)/shard_map/jit(_take)/gather | solution.py:62
  257.9 3.2 fusion
  261.1 0.0 copy-start
  261.1 2.2 copy-done
  263.3 1.6 constant_dynamic-slice_fusion
  264.8 1.2 collective-permute-start
  266.0 2.8 copy.12
  268.9 48.8 %collective-permute-done = bf16[768,1536]{0,1:T(8,128)(2,1)} collective-permute-done((bf16[768,1536]{0,1:T(8,128)(2,1)}, bf16[768,1536]{0,1:T(8,128)(2,1)}, u32[]{:S(2)}, u32[]{:S(2)}) %collective-permute-start) | collective-permute-done | bytes 2359328 | tf_op jit(solution)/shard_map/ppermute | solution.py:16
  317.6 5.3 %fusion.2 = f32[1,768,1536]{1,2,0:T(8,128)} fusion(bf16[768,1536]{0,1:T(8,128)(2,1)} %collective-permute-done, bf16[1,768,1536]{1,2,0:T(8,128)(2,1)S(1)} %copy.12, bf16[1536,1536]{0,1:T(8,128)(2,1)} %copy-done, s32[]{:T(128)S(6)} %select_n.72), kind=kLoop, calls=%fused_computation.8 | loop fusion | flops 5898240 | bytes 11796484 | tf_op jit(solution)/shard_map/broadcast_in_dim | solution.py:74
  322.9 6.0 %copy.15 = f32[1,768,1536]{2,1,0:T(8,128)} copy(f32[1,768,1536]{1,2,0:T(8,128)} %fusion.2) | data formatting | bytes 9437184
  (7 shorter events, 0.1 us)
Async XLA Ops:
  7.2 208.8 %all-gather.2.cloned.1.call-start = ((), (), s32[]{:S(2)}) async-start(), calls=%async_computation | async-start | bytes 12779520 | tf_op jit(solution)/shard_map/all_gather | solution.py:43
  261.1 2.2 copy-start
  264.8 52.8 %collective-permute-start = (bf16[768,1536]{0,1:T(8,128)(2,1)}, bf16[768,1536]{0,1:T(8,128)(2,1)}, u32[]{:S(2)}, u32[]{:S(2)}) collective-permute-start(bf16[768,1536]{0,1:T(8,128)(2,1)} %constant_dynamic-slice_fusion), channel_id=1, source_target_pairs={{0,64},{64,0},{128,192},{192,128},{1,65},{65,1},{129,193},{193,129... | collective-permute-start | bytes 7077896 | tf_op jit(solution)/shard_map/ppermute | solution.py:16
Sparse Core Ops, SparseCore 0:
  10.4 205.5 all-gather.1
where the time goes:
time: 337 us; the launch traced here: 336 us
  waiting for transfers between devices  253 us (75%)
  local copies, waits for them, and re-layouts  40.7 us (12%)
  other arithmetic  15.9 us (5%)
  between operations  14.1 us (4%)
  matrix products  10.4 us (3%)
    all_gather x1, waiting for transfers between devices, shards(): all_rows = lax.all_gather(factor, ('row', 'col'), axis=0, tiled=True)  205 us
    ppermute x1, waiting for transfers between devices, from_partner(): return lax.ppermute(block, axis, route)  48.8 us
    gather x2, local copies, waits for them, and re-layouts, shards(): jnp.take(schur.reshape(row_blocks, BLK, tile_cols), row_source, axis=0)  15.8 us
    gather x2, local copies, waits for them, and re-layouts, shards(): jnp.take(shaped.reshape(tile_rows, col_blocks, BLK), col_source, axis=1)  12.1 us
    unnamed x4, local copies, waits for them, and re-layouts  11.1 us
    dot_general x1, matrix products, shards(): lax.dot_general(row_side, col_side, contract, preferred_element_type=jnp....  8.18 us
  transfers between devices with their start and end apart: 2, of which 2 were waited for; matrix products, arithmetic and copies ran while one was open for 1% of the time, Pallas kernels for 0%

commit v1 on v0

v1 whole, which is shorter than its diff:
```python
import jax
import jax.numpy as jnp
from jax import lax
from jax.experimental import pallas as pl
from jax.experimental.pallas import tpu as pltpu
from jax.sharding import PartitionSpec as P

BLK = 256
MESH = pl.DeviceIdType.MESH


def local_source(map_ref, base, target, count):
    found = jnp.int32(0)
    for i in range(count):
        found = found + jnp.where(map_ref[0, base + i] == base + target, i, 0)
    return found


def prologue_kernel(map_ref, fill_ref, panel_ref, inverse_ref, front_ref, factor_ref, sent_ref, sems):
    row = lax.axis_index("row")
    col = lax.axis_index("col")
    parity = lax.axis_index("front") % 2
    per_tile = front_ref.shape[0]
    half = per_tile // 2
    copies = []
    for i in range(half):
        block = local_source(map_ref, row * per_tile, (1 - parity) * half + i, per_tile)
        copy = pltpu.make_async_copy(front_ref.at[block], sent_ref.at[i], sems.at[i])
        copy.start()
        copies.append(copy)
    size = inverse_ref.shape[0]
    upper = lax.broadcasted_iota(jnp.int32, (size, size), 0) <= lax.broadcasted_iota(
        jnp.int32, (size, size), 1
    )
    inverse = jnp.where(upper, inverse_ref[...].astype(jnp.float32), 0.0).astype(jnp.bfloat16)
    local_rows = panel_ref.shape[0]
    piece = 64
    shard = row * lax.axis_size("col") + col
    for t in range(local_rows // piece):
        block = (shard * local_rows + t * piece) // BLK
        keep = fill_ref[0, block].astype(jnp.float32)
        masked = (panel_ref[t * piece:(t + 1) * piece, :].astype(jnp.float32) * keep).astype(jnp.bfloat16)
        factor_ref[t * piece:(t + 1) * piece, :] = jnp.dot(
            masked, inverse, preferred_element_type=jnp.float32
        ).astype(jnp.bfloat16)
    for copy in copies:
        copy.wait()


def prologue(block_map, fill, panel, inverse, front_blocks):
    half = front_blocks.shape[0] // 2
    return pl.pallas_call(
        prologue_kernel,
        out_shape=(
            jax.ShapeDtypeStruct(panel.shape, jnp.bfloat16),
            jax.ShapeDtypeStruct((half,) + front_blocks.shape[1:], jnp.bfloat16),
        ),
        in_specs=[
            pl.BlockSpec(memory_space=pltpu.SMEM),
            pl.BlockSpec(memory_space=pltpu.SMEM),
            pl.BlockSpec(memory_space=pltpu.VMEM),
            pl.BlockSpec(memory_space=pltpu.VMEM),
            pl.BlockSpec(memory_space=pl.ANY),
        ],
        out_specs=(pl.BlockSpec(memory_space=pltpu.VMEM), pl.BlockSpec(memory_space=pl.ANY)),
        scratch_shapes=[pltpu.SemaphoreType.DMA((half,))],
        name="prologue",
    )(block_map, fill, panel, inverse, front_blocks)


def gather_kernel(own_ref, out_ref, local_sem, x_sem, row_recv, col_recv, row_send, chain_send, twin_send):
    front = lax.axis_index("front")
    row = lax.axis_index("row")
    col = lax.axis_index("col")
    zh, core = row // 2, row % 2
    y, zl = col // 2, col % 2
    partner = front + 1 - 2 * (front % 2)

    def device(f=None, zh_=None, core_=None, y_=None, zl_=None):
        return {
            "front": front if f is None else f,
            "row": (zh if zh_ is None else zh_) * 2 + (core if core_ is None else core_),
            "col": (y if y_ is None else y_) * 2 + (zl if zl_ is None else zl_),
        }

    y_up, y_down = (y + 1) % 4, (y + 3) % 4
    z_up, z_down = (zh + 1) % 4, (zh + 3) % 4

    barrier = pltpu.get_barrier_semaphore()
    peers = [
        device(f=partner),
        device(zl_=1 - zl),
        device(y_=y_up),
        device(y_=y_down),
        device(core_=1 - core),
    ]
    for other in (z_up, z_down):
        for k in range(2):
            peers.append(device(zh_=other, core_=k))
    for peer in peers:
        pl.semaphore_signal(barrier, inc=1, device_id=peer, device_id_type=MESH)
    pl.semaphore_wait(barrier, len(peers))

    distance = (zh - y + 4 + core * 2 * (y - zh)) % 4
    late = (core + zl) % 2
    step_of = distance + late
    at_home = zh == y
    is_source = jnp.logical_and(at_home, core == zl)
    is_twin = jnp.logical_and(at_home, core != zl)
    chained = jnp.logical_not(at_home)
    next_zh = (zh + 1 + 2 * core) % 4
    me = y * 2 + zl
    started = []

    def remote(cond, src, dst, send, recv, target):
        copy = pltpu.make_async_remote_copy(
            src_ref=src, dst_ref=dst, send_sem=send, recv_sem=recv, device_id=target, device_id_type=MESH
        )
        if cond is None:
            copy.start()
        else:
            pl.when(cond)(copy.start)
        started.append((cond, copy))

    def arrived(e, kind, j):
        sem = (row_recv if kind == 0 else col_recv).at[e, j]
        there = out_ref.at[2 * kind + e, j]
        pltpu.make_async_copy(there, there, sem).wait()

    def row_slot(e, j):
        return own_ref if (e == 0 and j is me) else out_ref.at[e, j]

    def send_row(e, n, j, target):
        remote(None, row_slot(e, j), out_ref.at[e, j], row_send.at[e, n], row_recv.at[e, j], target)

    def start_chain(e, j, zl_of):
        remote(
            is_source, row_slot(e, j), out_ref.at[2 + e, j], chain_send.at[e, j], col_recv.at[e, j],
            device(zh_=(zh + 1 + 2 * zl_of) % 4, core_=zl_of),
        )
        remote(
            is_source, row_slot(e, j), out_ref.at[2 + e, j], twin_send.at[e, j], col_recv.at[e, j],
            device(core_=1 - core),
        )

    def pass_chain(e, stage, n):
        if not 0 <= n - stage:
            return
        offsets = ((0,), (3, 1), (2,))[stage]
        here = jnp.logical_and(chained, step_of == n - stage)
        onward = jnp.logical_and(here, distance < 3)
        for dy in offsets:
            j = ((y + dy) % 4) * 2 + core
            pl.when(here)(lambda: arrived(e, 1, j))
            remote(
                onward, out_ref.at[2 + e, j], out_ref.at[2 + e, j], chain_send.at[e, j], col_recv.at[e, j],
                device(zh_=next_zh),
            )
            remote(
                here, out_ref.at[2 + e, j], out_ref.at[2 + e, j], twin_send.at[e, j], col_recv.at[e, j],
                device(core_=1 - core),
            )

    def level(e, n):
        other = 1 - zl
        if n == 0:
            if e == 1:
                arrived(1, 0, me)
            send_row(e, 0, me, device(zl_=other))
            send_row(e, 1, me, device(y_=y_up))
            send_row(e, 2, me, device(y_=y_down))
            start_chain(e, me, zl)
        if n == 1:
            j = y * 2 + other
            arrived(e, 0, j)
            send_row(e, 3, j, device(y_=y_up))
            send_row(e, 4, j, device(y_=y_down))
            start_chain(e, j, other)
        if n in (1, 2):
            side = zl if n == 1 else other
            down = y_down * 2 + side
            up = y_up * 2 + side
            arrived(e, 0, down)
            arrived(e, 0, up)
            send_row(e, 4 + n, ((y + 3 + 2 * side) % 4) * 2 + side, device(y_=(y + 1 + 2 * side) % 4))
            start_chain(e, down, side)
            start_chain(e, up, side)
        if n in (2, 3):
            side = zl if n == 2 else other
            far = ((y + 2) % 4) * 2 + side
            arrived(e, 0, far)
            start_chain(e, far, side)
        if n >= 1:
            for stage in range(3):
                if 1 <= n - stage <= 4:
                    pass_chain(e, stage, n)

    keep = pltpu.make_async_copy(own_ref, out_ref.at[0, me], local_sem)
    keep.start()
    remote(None, own_ref, out_ref.at[1, me], x_sem, row_recv.at[1, me], device(f=partner))
    lag = 2
    for g in range(7 + lag):
        if g < 7:
            level(0, g)
        if 0 <= g - lag:
            level(1, g - lag)

    for e in range(2):
        for j in range(8):
            pl.when(is_twin)(lambda: arrived(e, 1, jnp.int32(j)))
        for dy in range(4):
            pl.when(chained)(lambda: arrived(e, 1, ((y + dy) % 4) * 2 + (1 - core)))
    keep.wait()
    for cond, copy in started:
        if cond is None:
            copy.wait_send()
        else:
            pl.when(cond)(copy.wait_send)


def gather(factor):
    rows, depth = factor.shape
    return pl.pallas_call(
        gather_kernel,
        out_shape=jax.ShapeDtypeStruct((4, 8, rows, depth), jnp.bfloat16),
        in_specs=[pl.BlockSpec(memory_space=pl.ANY)],
        out_specs=pl.BlockSpec(memory_space=pl.ANY),
        scratch_shapes=[
            pltpu.SemaphoreType.DMA,
            pltpu.SemaphoreType.DMA,
            pltpu.SemaphoreType.DMA((2, 8)),
            pltpu.SemaphoreType.DMA((2, 8)),
            pltpu.SemaphoreType.DMA((2, 7)),
            pltpu.SemaphoreType.DMA((2, 8)),
            pltpu.SemaphoreType.DMA((2, 8)),
        ],
        compiler_params=pltpu.CompilerParams(collective_id=0, has_side_effects=True),
        cost_estimate=pl.CostEstimate(flops=0, bytes_accessed=150_000_000, transcendentals=0),
        name="gather",
    )(factor)


def finish_kernel(idx_ref, front_ref, came_ref, own_row_ref, far_row_ref, own_col_ref, far_col_ref, parent_ref, out_ref):
    contract = (((1,), (1,)), ((), ()))
    own_rows = own_row_ref[...]
    far_rows = far_row_ref[...]
    for b in range(6):
        own = pl.ds(pl.multiple_of(idx_ref[6 + b] * BLK, BLK), BLK)
        far = pl.ds(pl.multiple_of(idx_ref[12 + b] * BLK, BLK), BLK)
        here = slice(b * BLK, (b + 1) * BLK)
        update = lax.dot_general(own_rows, own_col_ref[own, :], contract, preferred_element_type=jnp.float32)
        mine = (front_ref[:, own].astype(jnp.float32) - update).astype(jnp.bfloat16)
        update = lax.dot_general(far_rows, far_col_ref[far, :], contract, preferred_element_type=jnp.float32)
        theirs = (came_ref[:, far].astype(jnp.float32) - update).astype(jnp.bfloat16)
        out_ref[:, here] = parent_ref[:, here].astype(jnp.float32) + (
            mine.astype(jnp.float32) + theirs.astype(jnp.float32)
        )


def finish(idx, front, came, factors, parent_front):
    tile = front.shape[1]
    depth = factors.shape[2]
    half = parent_front.shape[0]
    spec = pltpu.PrefetchScalarGridSpec(
        num_scalar_prefetch=1,
        grid=(half // BLK,),
        in_specs=[
            pl.BlockSpec((BLK, tile), lambda a, idx: (idx[a], 0)),
            pl.BlockSpec((BLK, tile), lambda a, idx: (a, 0)),
            pl.BlockSpec((None, BLK, depth), lambda a, idx: (0, idx[a], 0)),
            pl.BlockSpec((None, BLK, depth), lambda a, idx: (1, idx[3 + a], 0)),
            pl.BlockSpec((None, tile, depth), lambda a, idx: (idx[18], 0, 0)),
            pl.BlockSpec((None, tile, depth), lambda a, idx: (idx[18] + 1, 0, 0)),
            pl.BlockSpec((BLK, tile), lambda a, idx: (a, 0)),
        ],
        out_specs=pl.BlockSpec((BLK, tile), lambda a, idx: (a, 0)),
    )
    return pl.pallas_call(
        finish_kernel,
        grid_spec=spec,
        out_shape=jax.ShapeDtypeStruct((half, tile), jnp.float32),
        compiler_params=pltpu.CompilerParams(vmem_limit_bytes=40 * 2**20),
        cost_estimate=pl.CostEstimate(flops=4 * half * tile * depth, bytes_accessed=20_000_000, transcendentals=0),
        name="finish",
    )(idx, front, came, factors, factors, factors, factors, parent_front)


def swap_pairs(block, axis):
    count = lax.axis_size(axis)
    return lax.ppermute(block, axis, [(i, i ^ 1) for i in range(count)])


def group_source(mapping, start, count):
    group = lax.dynamic_slice_in_dim(mapping, start, count, 0) - start
    target = jnp.arange(count, dtype=jnp.int32)
    return jnp.sum((group[:, None] == target[None, :]).astype(jnp.int32) * target[:, None], axis=0)


def shards(front, panel, inverse, fill, block_map, parent_front):
    row = lax.axis_index("row")
    col = lax.axis_index("col")
    parity = lax.axis_index("front") % 2
    tile = front.shape[1]
    per_tile = tile // BLK
    half = per_tile // 2
    far_map = swap_pairs(block_map[0], "front")
    factor, sent = prologue(block_map, fill, panel[0], inverse[0], front.reshape(per_tile, BLK, tile))
    came = swap_pairs(sent, "front")
    gathered = gather(factor).reshape(4, tile, factor.shape[1])
    picks = [
        lax.dynamic_slice_in_dim(group_source(m, row * per_tile, per_tile), parity * half, half, 0)
        for m in (block_map[0], far_map)
    ]
    picks += [group_source(m, col * per_tile, per_tile) for m in (block_map[0], far_map)]
    home = jnp.logical_and(row // 2 == col // 2, row % 2 == col % 2)
    picks.append(jnp.where(home, 0, 2).astype(jnp.int32)[None])
    idx = jnp.concatenate(picks)
    parent = finish(idx, front[0], came.reshape(half * BLK, tile), gathered, parent_front[0])
    return (factor[None], parent[None])


def solution(mesh):
    placed = (
        P("front", "row", "col"),
        P("front", ("row", "col"), None),
        P("front", None, None),
        P("front", None),
        P("front", None),
        P("front", "row", "col"),
    )
    return jax.shard_map(
        shards,
        mesh=mesh,
        in_specs=placed,
        out_specs=(P("front", ("row", "col"), None), P("front", "row", "col")),
        check_vma=False,
    )
```

time: 337 us -> 196 us (0.58)
  the two profiles are of different devices: /device:TPU:105 before, /device:TPU:41 now
where the time goes in v1:
time: 196 us
  Pallas kernels  190 us (97%)
  local copies, waits for them, and re-layouts  2.58 us (1%)
    pallas_call x1, Pallas kernels, gather(): pl.pallas_call(gather_kernel, out_shape=jax.ShapeDtypeStruct((4, 8, rows,...  108 us
    pallas_call x1, Pallas kernels, prologue(): pl.pallas_call(prologue_kernel, out_shape=(jax.ShapeDtypeStruct(panel.sha...  74.6 us
    pallas_call x1, Pallas kernels, finish(): pl.pallas_call(finish_kernel, grid_spec=spec, out_shape=jax.ShapeDtypeStr...  8.2 us
  transfers between devices with their start and end apart: 2, of which 0 were waited for; matrix products, arithmetic and copies ran while one was open for 0% of the time, Pallas kernels for 55%

profile of v1, /device:TPU:41, one launch (start us, length us, event | category | flops | bytes accessed | tf_op | source)
XLA Modules:
  0.0 195.6 jit_solution(1716481176662706471)
XLA Ops:
  0.6 0.0 copy-start.2
  0.6 0.0 copy-start.1
  0.7 74.6 %prologue.1 = (bf16[192,512]{1,0:T(8,128)(2,1)}, bf16[3,256,1536]{2,1,0:T(8,128)(2,1)}) custom-call(s32[1,48]{1,0:T(1,128)} %map_ref.1, s32[1,48]{1,0:T(1,128)} %fill_ref.1, bf16[192,512]{1,0:T(8,128)(2,1)} %bitcast.24, bf16[512,512]{1,0:T(8,128)(2,1)} %bitcast.23, bf16[6,256,1536]{2,1,0:T(8,128)(2,1)} %bitcast.15), custom_call_target="tpu_custom_call" | custom-call | tf_op jit(solution)/shard_map/prologue/pallas_call | solution.py:52
  75.3 1.3 collective-permute-start.1
  76.6 0.0 copy-done.2
  76.6 0.3 collective-permute-start
  76.8 0.1 subtract_bitcast_fusion
  76.9 0.1 select_reduce_fusion.3
  77.0 107.5 %gather.1 = bf16[4,8,192,512]{3,2,1,0:T(8,128)(2,1)} custom-call(bf16[192,512]{1,0:T(8,128)(2,1)} %get-tuple-element.4.own_ref), custom_call_target="tpu_custom_call" | custom-call | bytes 150000000 | tf_op jit(solution)/shard_map/gather/pallas_call | solution.py:223
  184.5 0.1 dynamic_slice.19
  184.6 0.0 collective-permute-done
  184.6 0.1 dynamic-slice_subtract_fusion
  184.7 0.1 select_reduce_fusion.2
  184.8 0.1 dynamic_slice.21
  184.8 0.1 select_reduce_fusion
  184.9 0.1 concatenate.3.idx_ref
  185.0 0.0 collective-permute-done.1
  185.0 0.0 copy-done.1
  185.0 0.0 copy-start
  185.0 2.3 %copy-done = bf16[1,1536,1536]{2,1,0:T(8,128)(2,1)S(1)} copy-done((bf16[1,1536,1536]{2,1,0:T(8,128)(2,1)S(1)}, bf16[1,1536,1536]{2,1,0:T(8,128)(2,1)}, u32[]{:S(2)}) %copy-start) | copy-done | bytes 4718616
  187.4 8.2 %finish.1 = f32[768,1536]{1,0:T(8,128)} custom-call(s32[19]{0:T(128)S(1)} %concatenate.3.idx_ref, bf16[1536,1536]{1,0:T(8,128)(2,1)S(1)} %bitcast.16, bf16[768,1536]{1,0:T(8,128)(2,1)} %bitcast.9.came_ref, bf16[4,1536,512]{2,1,0:T(8,128)(2,1)} %bitcast.18, bf16[4,1536,512]{2,1,0:T(8,128)(2,1)} %bitcast.19, bf16[4,1536,512]{2,1,0:T(8,128)(2,1)} %bitcast.20, ...), custom_call_target="tpu_custom_call" | custom-call | flops 2415919104 | bytes 20000000 | tf_op jit(solution)/shard_map/finish/pallas_call | solution.py:278
Async XLA Ops:
  0.6 75.9 %copy-start.2 = (s32[1,48]{1,0:T(1,128)S(1)}, s32[1,48]{1,0:T(1,128)}, u32[]{:S(2)}) copy-start(s32[1,48]{1,0:T(1,128)} %map_ref.1) | copy-start | bytes 580
  0.6 184.4 %copy-start.1 = (bf16[1,768,1536]{2,1,0:T(8,128)(2,1)S(1)}, bf16[1,768,1536]{2,1,0:T(8,128)(2,1)}, u32[]{:S(2)}) copy-start(bf16[1,768,1536]{2,1,0:T(8,128)(2,1)} %param.11) | copy-start | bytes 7077892
  75.3 109.8 %collective-permute-start.1 = (bf16[3,256,1536]{2,1,0:T(8,128)(2,1)}, bf16[3,256,1536]{2,1,0:T(8,128)(2,1)}, u32[]{:S(2)}, u32[]{:S(2)}) collective-permute-start(bf16[3,256,1536]{2,1,0:T(8,128)(2,1)} %get-tuple-element.5), channel_id=1, source_target_pairs={{0,64},{64,0},{128,192},{192,128},{1,65},{65,1},{129,193},{193,129... | collective-permute-start | bytes 7077896 | tf_op jit(solution)/shard_map/ppermute | solution.py:290
  76.6 108.0 %collective-permute-start = (s32[48]{0:T(128)S(1)}, s32[48]{0:T(128)S(1)}, u32[]{:S(2)}, u32[]{:S(2)}) collective-permute-start(s32[48]{0:T(128)S(1)} %bitcast.26), channel_id=1, source_target_pairs={{0,64},{64,0},{128,192},{192,128},{1,65},{65,1},{129,193},{193,129... | collective-permute-start | bytes 584 | tf_op jit(solution)/shard_map/ppermute | solution.py:290
  185.0 2.3 %copy-start = (bf16[1,1536,1536]{2,1,0:T(8,128)(2,1)S(1)}, bf16[1,1536,1536]{2,1,0:T(8,128)(2,1)}, u32[]{:S(2)}) copy-start(bf16[1,1536,1536]{2,1,0:T(8,128)(2,1)} %param.6) | copy-start | bytes 14155780

commit v2 on v0

v2 whole, which is shorter than its diff:
```python
import jax
import jax.numpy as jnp
from jax import lax
from jax.experimental import pallas as pl
from jax.experimental.pallas import tpu as pltpu
from jax.sharding import PartitionSpec as P

BLK = 256
MESH = pl.DeviceIdType.MESH


def local_source(map_ref, base, target, count):
    found = jnp.int32(0)
    for i in range(count):
        found = found + jnp.where(map_ref[0, base + i] == base + target, i, 0)
    return jnp.clip(found, 0, count - 1)


def kernel(
    map_ref, fill_ref, map_any, panel_any, inverse_any, front_any, parent_any,
    factor_ref, base,
    tiles, front_v, sent, came, update, parent_v, panel_v, inverse_v, far_v, far_map,
    load_sem, far_sem, map_sems, x_sem, front_send, front_recv,
    row_recv, col_recv, row_send, chain_send, twin_send,
):
    front = lax.axis_index("front")
    row = lax.axis_index("row")
    col = lax.axis_index("col")
    zh, core = row // 2, row % 2
    y, zl = col // 2, col % 2
    parity = front % 2
    partner = front + 1 - 2 * parity
    per_tile = front_v.shape[0]
    half = per_tile // 2
    local_rows = panel_v.shape[0]
    fine = tiles.shape[2]
    pieces = local_rows // fine
    per_block = BLK // fine

    def device(f=None, zh_=None, core_=None, y_=None, zl_=None):
        return {
            "front": front if f is None else f,
            "row": (zh if zh_ is None else zh_) * 2 + (core if core_ is None else core_),
            "col": (y if y_ is None else y_) * 2 + (zl if zl_ is None else zl_),
        }

    barrier = pltpu.get_barrier_semaphore()
    peers = [device(f=partner), device(zl_=1 - zl), device(core_=1 - core)]
    peers += [device(y_=(y + n) % 4) for n in (1, 3)]
    peers += [device(zh_=(zh + n) % 4, core_=k) for n in (1, 3) for k in range(2)]
    for peer in peers:
        pl.semaphore_signal(barrier, inc=1, device_id=peer, device_id_type=MESH)

    loads = [
        pltpu.make_async_copy(panel_any, panel_v, load_sem.at[0]),
        pltpu.make_async_copy(inverse_any, inverse_v, load_sem.at[1]),
        pltpu.make_async_copy(parent_any, parent_v, load_sem.at[2]),
    ] + [
        pltpu.make_async_copy(front_any.at[:, :, pl.ds(b * BLK, BLK)], front_v.at[:, b], load_sem.at[3 + b])
        for b in range(per_tile)
    ]
    for load in loads:
        load.start()

    at_home = zh == y
    is_source = jnp.logical_and(at_home, core == zl)
    is_twin = jnp.logical_and(at_home, core != zl)
    chained = jnp.logical_not(at_home)
    distance = (zh - y + 4 + core * 2 * (y - zh)) % 4
    onward = jnp.logical_and(chained, distance < 3)
    next_zh = (zh + 1 + 2 * core) % 4
    other = 1 - zl
    me = y * 2 + zl
    across = y * 2 + other

    def slot(kind, j):
        return tiles.at[kind, pl.ds(j * pieces, pieces)]

    loads[0].wait()
    loads[1].wait()
    size = inverse_v.shape[0]
    upper = lax.broadcasted_iota(jnp.int32, (size, size), 0) <= lax.broadcasted_iota(
        jnp.int32, (size, size), 1
    )
    inverse = jnp.where(upper, inverse_v[...].astype(jnp.float32), 0.0).astype(jnp.bfloat16)
    piece = 64
    shard = row * lax.axis_size("col") + col
    for t in range(local_rows // piece):
        block = (shard * local_rows + t * piece) // BLK
        keep = fill_ref[0, block].astype(jnp.float32)
        masked = (panel_v[t * piece:(t + 1) * piece, :].astype(jnp.float32) * keep).astype(jnp.bfloat16)
        rows = jnp.dot(masked, inverse, preferred_element_type=jnp.float32).astype(jnp.bfloat16)
        factor_ref[t * piece:(t + 1) * piece, :] = rows
        for q in range(piece // fine):
            tiles[0, me * pieces + t * (piece // fine) + q] = rows[q * fine:(q + 1) * fine]

    row_first = row * per_tile
    col_first = col * per_tile
    for load in loads[3:]:
        load.wait()
    for i in range(half):
        block = local_source(map_ref, row_first, (1 - parity) * half + i, per_tile)
        for b in range(per_tile):
            sent[i, b] = front_v[block, local_source(map_ref, col_first, b, per_tile)]

    pl.semaphore_wait(barrier, len(peers))

    started = []

    def remote(cond, src, dst, send, recv, target):
        copy = pltpu.make_async_remote_copy(
            src_ref=src, dst_ref=dst, send_sem=send, recv_sem=recv, device_id=target, device_id_type=MESH
        )
        if cond is None:
            copy.start()
        else:
            pl.when(cond)(copy.start)
        started.append((cond, copy))
        return copy

    parts = 2

    def part(kind, j, h):
        return tiles.at[kind, pl.ds(j * pieces + h * (pieces // parts), pieces // parts)]

    def arrived(e, kind, j):
        sem = row_recv.at[e, j] if kind == 0 else col_recv.at[e, j, 0]
        there = slot(2 * kind + e, j)
        pltpu.make_async_copy(there, there, sem).wait()

    def spread(e, n, j, target):
        remote(None, slot(e, j), slot(e, j), row_send.at[e, n], row_recv.at[e, j], target)

    def own(e):
        spread(e, 0, me, device(zl_=other))
        spread(e, 1, me, device(y_=(y + 1) % 4))
        spread(e, 2, me, device(y_=(y + 3) % 4))
        start_chain(e, me, True)

    def cross(e):
        arrived(e, 0, across)
        spread(e, 3, across, device(y_=(y + 1) % 4))
        spread(e, 4, across, device(y_=(y + 3) % 4))
        start_chain(e, across, False)

    def relay(e, near):
        side = zl if near else other
        down = ((y + 3) % 4) * 2 + side
        up = ((y + 1) % 4) * 2 + side
        arrived(e, 0, down)
        arrived(e, 0, up)
        spread(
            e, 5 if near else 6, ((y + 3 + 2 * side) % 4) * 2 + side, device(y_=(y + 1 + 2 * side) % 4)
        )
        start_chain(e, down, near)
        start_chain(e, up, near)

    def last(e, near):
        j = ((y + 2) % 4) * 2 + (zl if near else other)
        pl.when(is_source)(lambda: arrived(e, 0, j))
        start_chain(e, j, near)

    in_flight = {}

    def start_chain(e, j, near):
        side = zl if near else other
        for h in range(parts):
            if (near, h) in in_flight:
                before = in_flight[near, h]
                pl.when(is_source)(before.wait_send)
                started[:] = [item for item in started if item[1] is not before]
            in_flight[near, h] = remote(
                is_source, part(e, j, h), part(2 + e, j, h), chain_send.at[e, j, h], col_recv.at[e, j, h],
                device(zh_=(zh + 1 + 2 * side) % 4, core_=side),
            )
        remote(
            is_source, slot(e, j), slot(2 + e, j), twin_send.at[e, j], col_recv.at[e, j, 0], device(core_=1 - core)
        )

    def pass_chain(e, dy):
        j = ((y + dy) % 4) * 2 + core
        for h in range(parts):
            here = part(2 + e, j, h)
            pl.when(chained)(pltpu.make_async_copy(here, here, col_recv.at[e, j, h]).wait)
            remote(onward, here, here, chain_send.at[e, j, h], col_recv.at[e, j, h], device(zh_=next_zh))
        here = slot(2 + e, j)
        remote(chained, here, here, twin_send.at[e, j], col_recv.at[e, j, 0], device(core_=1 - core))

    tell = pltpu.make_async_remote_copy(
        src_ref=map_any, dst_ref=far_v, send_sem=map_sems.at[0], recv_sem=map_sems.at[1],
        device_id=device(f=partner), device_id_type=MESH,
    )
    tell.start()
    exchange = pltpu.make_async_remote_copy(
        src_ref=slot(0, me), dst_ref=slot(1, me), send_sem=x_sem, recv_sem=row_recv.at[1, me],
        device_id=device(f=partner), device_id_type=MESH,
    )
    exchange.start()
    fronts = []
    for i in range(half):
        fronts.append(pltpu.make_async_remote_copy(
            src_ref=sent.at[i], dst_ref=came.at[i], send_sem=front_send.at[i],
            recv_sem=front_recv.at[i], device_id=device(f=partner), device_id_type=MESH,
        ))
        fronts[i].start()

    own(0)
    cross(0)
    relay(0, True)
    arrived(1, 0, me)
    own(1)
    relay(0, False)
    pass_chain(0, 0)
    cross(1)
    last(0, True)
    pass_chain(0, 3)
    relay(1, True)
    last(0, False)
    pass_chain(0, 1)
    pass_chain(0, 2)
    relay(1, False)
    pass_chain(1, 0)
    last(1, True)
    last(1, False)
    for dy in (3, 1, 2):
        pass_chain(1, dy)

    tell.wait()
    far_copy = pltpu.make_async_copy(far_v, far_map, far_sem)
    far_copy.start()
    far_copy.wait()
    exchange.wait_send()
    for e in range(2):
        for j in range(8):
            pl.when(is_twin)(lambda: arrived(e, 1, jnp.int32(j)))
        for dy in range(4):
            pl.when(chained)(lambda: arrived(e, 1, ((y + dy) % 4) * 2 + (1 - core)))
        for side in range(2):
            pl.when(jnp.logical_not(is_source))(lambda: arrived(e, 0, ((y + 2) % 4) * 2 + side))

    loads[2].wait()
    col_kind = jnp.where(is_source, 0, 2)
    contract = (((1,), (1,)), ((), ()))

    def take(kind, block):
        return jnp.concatenate([tiles[kind, block * per_block + q] for q in range(per_block)], axis=0)

    def products(e, maps, use):
        for a in range(half):
            block = local_source(maps, row_first, parity * half + a, per_tile)
            rows = take(e, block)
            for b in range(per_tile):
                source = local_source(maps, col_first, b, per_tile)
                cols = take(col_kind + e, source)
                use(a, b, block, source, lax.dot_general(rows, cols, contract, preferred_element_type=jnp.float32))

    def use_own(a, b, block, source, product):
        entries = front_v[block, source]
        mine = (entries.astype(jnp.float32) - product).astype(jnp.bfloat16).astype(jnp.float32)
        base[a, :, b * BLK:(b + 1) * BLK] = parent_v[a, :, b * BLK:(b + 1) * BLK].astype(jnp.float32) + mine

    def use_far(a, b, block, source, product):
        update[a, :, b * BLK:(b + 1) * BLK] = product

    products(0, map_ref, use_own)
    products(1, far_map, use_far)

    for a in range(half):
        fronts[a].wait()
        for b in range(per_tile):
            entries = came[a, b]
            where = slice(b * BLK, (b + 1) * BLK)
            theirs = (entries.astype(jnp.float32) - update[a, :, where]).astype(jnp.bfloat16)
            base[a, :, where] = base[a, :, where] + theirs.astype(jnp.float32)
    for cond, copy in started:
        if cond is None:
            copy.wait_send()
        else:
            pl.when(cond)(copy.wait_send)


def shards(front, panel, inverse, fill, block_map, parent_front):
    tile = front.shape[1]
    per_tile = tile // BLK
    half = per_tile // 2
    local_rows, depth = panel.shape[1:]
    anywhere = pl.BlockSpec(memory_space=pl.ANY)
    dma = pltpu.SemaphoreType.DMA
    bf16, f32 = jnp.bfloat16, jnp.float32
    factor, parent = pl.pallas_call(
        kernel,
        out_shape=(
            jax.ShapeDtypeStruct((local_rows, depth), bf16),
            pltpu.VMEM((half, BLK, tile), f32),
        ),
        in_specs=[pl.BlockSpec(memory_space=pltpu.SMEM)] * 2 + [anywhere] * 5,
        out_specs=(pl.BlockSpec(memory_space=pltpu.VMEM), pl.BlockSpec(memory_space=pltpu.VMEM)),
        scratch_shapes=[
            pltpu.VMEM((4, tile // 32, 32, depth), bf16),
            pltpu.VMEM((per_tile, per_tile, BLK, BLK), bf16),
            pltpu.VMEM((half, per_tile, BLK, BLK), bf16),
            pltpu.VMEM((half, per_tile, BLK, BLK), bf16),
            pltpu.VMEM((half, BLK, tile), f32),
            pltpu.VMEM((half, BLK, tile), bf16),
            pltpu.VMEM((local_rows, depth), bf16),
            pltpu.VMEM((depth, depth), bf16),
            pltpu.VMEM(block_map.shape, jnp.int32),
            pltpu.SMEM(block_map.shape, jnp.int32),
            dma((3 + per_tile,)), dma, dma((2,)), dma, dma((half,)), dma((half,)),
            dma((2, 8)), dma((2, 8, 2)), dma((2, 7)), dma((2, 8, 2)), dma((2, 8)),
        ],
        compiler_params=pltpu.CompilerParams(
            collective_id=0, has_side_effects=True, vmem_limit_bytes=56 * 2**20
        ),
        name="panel_and_extend_add",
    )(
        block_map, fill, block_map, panel[0], inverse[0], front.reshape(per_tile, BLK, tile),
        parent_front.reshape(half, BLK, tile),
    )
    return (factor[None], parent.reshape(1, half * BLK, tile))


def solution(mesh):
    placed = (
        P("front", "row", "col"),
        P("front", ("row", "col"), None),
        P("front", None, None),
        P("front", None),
        P("front", None),
        P("front", "row", "col"),
    )
    return jax.shard_map(
        shards,
        mesh=mesh,
        in_specs=placed,
        out_specs=(P("front", ("row", "col"), None), P("front", "row", "col")),
        check_vma=False,
    )
```

time: 337 us -> 79 us (0.23)
  the two profiles are of different devices: /device:TPU:105 before, /device:TPU:41 now
where the time goes in v2:
time: 79 us; the launch traced here: 78.9 us
  Pallas kernels  75.4 us (95%)
  local copies, waits for them, and re-layouts  2.87 us (4%)
    pallas_call x1, Pallas kernels, shards(): pl.pallas_call(kernel, out_shape=(jax.ShapeDtypeStruct((local_rows, depth...  75.4 us
    unnamed x4, local copies, waits for them, and re-layouts  2.87 us

profile of v2, /device:TPU:41, one launch (start us, length us, event | category | flops | bytes accessed | tf_op | source)
XLA Modules:
  0.0 78.9 jit_solution(9805676043937675362)
XLA Ops:
  0.6 75.4 %panel_and_extend_add.1 = (bf16[192,512]{1,0:T(8,128)(2,1)}, f32[3,256,1536]{2,1,0:T(8,128)S(1)}) custom-call(s32[1,48]{1,0:T(1,128)} %map_any.1, s32[1,48]{1,0:T(1,128)} %fill_ref.1, s32[1,48]{1,0:T(1,128)} %map_any.1, bf16[192,512]{1,0:T(8,128)(2,1)} %bitcast.11, bf16[512,512]{1,0:T(8,128)(2,1)} %bitcast.9, bf16[6,256,1536]{2,1,0:T(8,128)(2,1)} %bitcast.7, ...), custom_call_target="tpu_custom_call" | custom-call | tf_op jit(solution)/shard_map/panel_and_extend_add/pallas_call | solution.py:290
  76.0 0.0 copy-start
  76.0 2.2 %copy.10 = f32[1,768,1536]{2,1,0:T(8,128)} copy(f32[1,768,1536]{2,1,0:T(8,128)S(1)} %bitcast.6) | data formatting | bytes 9437184
  78.2 0.0 copy-done
  78.2 0.7 copy.11
Async XLA Ops:
  76.0 2.2 %copy-start = (bf16[192,512]{1,0:T(8,128)(2,1)S(1)}, bf16[192,512]{1,0:T(8,128)(2,1)}, u32[]{:S(2)}) copy-start(bf16[192,512]{1,0:T(8,128)(2,1)} %get-tuple-element.4) | copy-start | bytes 589828

commit v3 on v2

--- a/solution.py
+++ b/solution.py
@@ -19,7 +19,7 @@
 def kernel(
     map_ref, fill_ref, map_any, panel_any, inverse_any, front_any, parent_any,
     factor_ref, base,
-    tiles, front_v, sent, came, update, parent_v, panel_v, inverse_v, far_v, far_map,
+    own_tiles, far_tiles, front_v, sent, came, parent_v, panel_v, inverse_v, far_v, far_map,
     load_sem, far_sem, map_sems, x_sem, front_send, front_recv,
     row_recv, col_recv, row_send, chain_send, twin_send,
 ):
@@ -33,7 +33,8 @@
     per_tile = front_v.shape[0]
     half = per_tile // 2
     local_rows = panel_v.shape[0]
-    fine = tiles.shape[2]
+    tiles = (own_tiles, far_tiles)
+    fine = own_tiles.shape[2]
     pieces = local_rows // fine
     per_block = BLK // fine
 
@@ -74,7 +75,7 @@
     across = y * 2 + other
 
     def slot(kind, j):
-        return tiles.at[kind, pl.ds(j * pieces, pieces)]
+        return tiles[kind % 2].at[kind // 2, pl.ds(j * pieces, pieces)]
 
     loads[0].wait()
     loads[1].wait()
@@ -92,7 +93,7 @@
         rows = jnp.dot(masked, inverse, preferred_element_type=jnp.float32).astype(jnp.bfloat16)
         factor_ref[t * piece:(t + 1) * piece, :] = rows
         for q in range(piece // fine):
-            tiles[0, me * pieces + t * (piece // fine) + q] = rows[q * fine:(q + 1) * fine]
+            own_tiles[0, me * pieces + t * (piece // fine) + q] = rows[q * fine:(q + 1) * fine]
 
     row_first = row * per_tile
     col_first = col * per_tile
@@ -118,10 +119,10 @@
         started.append((cond, copy))
         return copy
 
-    parts = 2
+    parts = 4
 
     def part(kind, j, h):
-        return tiles.at[kind, pl.ds(j * pieces + h * (pieces // parts), pieces // parts)]
+        return tiles[kind % 2].at[kind // 2, pl.ds(j * pieces + h * (pieces // parts), pieces // parts)]
 
     def arrived(e, kind, j):
         sem = row_recv.at[e, j] if kind == 0 else col_recv.at[e, j, 0]
@@ -135,13 +136,11 @@
         spread(e, 0, me, device(zl_=other))
         spread(e, 1, me, device(y_=(y + 1) % 4))
         spread(e, 2, me, device(y_=(y + 3) % 4))
-        start_chain(e, me, True)
 
     def cross(e):
         arrived(e, 0, across)
         spread(e, 3, across, device(y_=(y + 1) % 4))
         spread(e, 4, across, device(y_=(y + 3) % 4))
-        start_chain(e, across, False)
 
     def relay(e, near):
         side = zl if near else other
@@ -152,30 +151,32 @@
         spread(
             e, 5 if near else 6, ((y + 3 + 2 * side) % 4) * 2 + side, device(y_=(y + 1 + 2 * side) % 4)
         )
-        start_chain(e, down, near)
-        start_chain(e, up, near)
-
-    def last(e, near):
-        j = ((y + 2) % 4) * 2 + (zl if near else other)
-        pl.when(is_source)(lambda: arrived(e, 0, j))
-        start_chain(e, j, near)
-
-    in_flight = {}
-
-    def start_chain(e, j, near):
+
+    in_flight = {True: [], False: []}
+
+    def feed(e, j, near):
         side = zl if near else other
+        queue = in_flight[near]
         for h in range(parts):
-            if (near, h) in in_flight:
-                before = in_flight[near, h]
-                pl.when(is_source)(before.wait_send)
-                started[:] = [item for item in started if item[1] is not before]
-            in_flight[near, h] = remote(
-                is_source, part(e, j, h), part(2 + e, j, h), chain_send.at[e, j, h], col_recv.at[e, j, h],
-                device(zh_=(zh + 1 + 2 * side) % 4, core_=side),
+            for near_zl, lag in enumerate((4, 2)):
+                if len(queue) >= lag:
+                    pl.when(jnp.logical_and(is_source, zl == near_zl))(queue[-lag].wait_send)
+            copy = pltpu.make_async_remote_copy(
+                src_ref=part(e, j, h), dst_ref=part(2 + e, j, h), send_sem=chain_send.at[e, j, h],
+                recv_sem=col_recv.at[e, j, h], device_id=device(zh_=(zh + 1 + 2 * side) % 4, core_=side),
+                device_id_type=MESH,
             )
+            pl.when(is_source)(copy.start)
+            queue.append(copy)
         remote(
             is_source, slot(e, j), slot(2 + e, j), twin_send.at[e, j], col_recv.at[e, j, 0], device(core_=1 - core)
         )
+
+    def feed_from(e, dy, near):
+        j = ((y + dy) % 4) * 2 + (zl if near else other)
+        if dy == 2:
+            pl.when(is_source)(lambda: arrived(e, 0, j))
+        feed(e, j, near)
 
     def pass_chain(e, dy):
         j = ((y + dy) % 4) * 2 + core
@@ -205,24 +206,32 @@
         fronts[i].start()
 
     own(0)
+    feed_from(0, 0, True)
     cross(0)
+    feed_from(0, 0, False)
     relay(0, True)
+    feed_from(0, 3, True)
     arrived(1, 0, me)
     own(1)
     relay(0, False)
+    feed_from(0, 3, False)
     pass_chain(0, 0)
+    feed_from(0, 1, True)
+    feed_from(0, 1, False)
     cross(1)
-    last(0, True)
+    feed_from(0, 2, True)
     pass_chain(0, 3)
+    feed_from(0, 2, False)
     relay(1, True)
-    last(0, False)
+    feed_from(1, 0, True)
     pass_chain(0, 1)
+    feed_from(1, 0, False)
     pass_chain(0, 2)
     relay(1, False)
-    pass_chain(1, 0)
-    last(1, True)
-    last(1, False)
     for dy in (3, 1, 2):
+        feed_from(1, dy, True)
+        feed_from(1, dy, False)
+    for dy in (0, 3, 1, 2):
         pass_chain(1, dy)
 
     tell.wait()
@@ -230,7 +239,33 @@
     far_copy.start()
     far_copy.wait()
     exchange.wait_send()
-    for e in range(2):
+    loads[2].wait()
+    col_kind = jnp.where(is_source, 0, 1)
+    contract = (((1,), (1,)), ((), ()))
+
+    def take(e, kind, block):
+        return jnp.concatenate([tiles[e][kind, block * per_block + q] for q in range(per_block)], axis=0)
+
+    def products(e, maps, use):
+        for a in range(half):
+            block = local_source(maps, row_first, parity * half + a, per_tile)
+            rows = take(e, 0, block)
+            for b in range(per_tile):
+                source = local_source(maps, col_first, b, per_tile)
+                cols = take(e, col_kind, source)
+                use(a, b, block, source, lax.dot_general(rows, cols, contract, preferred_element_type=jnp.float32))
+
+    def use_own(a, b, block, source, product):
+        entries = front_v[block, source]
+        mine = (entries.astype(jnp.float32) - product).astype(jnp.bfloat16).astype(jnp.float32)
+        base[a, :, b * BLK:(b + 1) * BLK] = parent_v[a, :, b * BLK:(b + 1) * BLK].astype(jnp.float32) + mine
+
+    def use_far(a, b, block, source, product):
+        where = slice(b * BLK, (b + 1) * BLK)
+        theirs = (came[a, b].astype(jnp.float32) - product).astype(jnp.bfloat16)
+        base[a, :, where] = base[a, :, where] + theirs.astype(jnp.float32)
+
+    def settle(e):
         for j in range(8):
             pl.when(is_twin)(lambda: arrived(e, 1, jnp.int32(j)))
         for dy in range(4):
@@ -238,40 +273,17 @@
         for side in range(2):
             pl.when(jnp.logical_not(is_source))(lambda: arrived(e, 0, ((y + 2) % 4) * 2 + side))
 
-    loads[2].wait()
-    col_kind = jnp.where(is_source, 0, 2)
-    contract = (((1,), (1,)), ((), ()))
-
-    def take(kind, block):
-        return jnp.concatenate([tiles[kind, block * per_block + q] for q in range(per_block)], axis=0)
-
-    def products(e, maps, use):
-        for a in range(half):
-            block = local_source(maps, row_first, parity * half + a, per_tile)
-            rows = take(e, block)
-            for b in range(per_tile):
-                source = local_source(maps, col_first, b, per_tile)
-                cols = take(col_kind + e, source)
-                use(a, b, block, source, lax.dot_general(rows, cols, contract, preferred_element_type=jnp.float32))
-
-    def use_own(a, b, block, source, product):
-        entries = front_v[block, source]
-        mine = (entries.astype(jnp.float32) - product).astype(jnp.bfloat16).astype(jnp.float32)
-        base[a, :, b * BLK:(b + 1) * BLK] = parent_v[a, :, b * BLK:(b + 1) * BLK].astype(jnp.float32) + mine
-
-    def use_far(a, b, block, source, product):
-        update[a, :, b * BLK:(b + 1) * BLK] = product
-
+    settle(0)
     products(0, map_ref, use_own)
+    for copy in fronts:
+        copy.wait()
+    settle(1)
     products(1, far_map, use_far)
 
-    for a in range(half):
-        fronts[a].wait()
-        for b in range(per_tile):
-            entries = came[a, b]
-            where = slice(b * BLK, (b + 1) * BLK)
-            theirs = (entries.astype(jnp.float32) - update[a, :, where]).astype(jnp.bfloat16)
-            base[a, :, where] = base[a, :, where] + theirs.astype(jnp.float32)
+    for queue in in_flight.values():
+        for near_zl, lag in enumerate((4, 2)):
+            for copy in queue[-lag:]:
+                pl.when(jnp.logical_and(is_source, zl == near_zl))(copy.wait_send)
     for cond, copy in started:
         if cond is None:
             copy.wait_send()
@@ -296,18 +308,18 @@
         in_specs=[pl.BlockSpec(memory_space=pltpu.SMEM)] * 2 + [anywhere] * 5,
         out_specs=(pl.BlockSpec(memory_space=pltpu.VMEM), pl.BlockSpec(memory_space=pltpu.VMEM)),
         scratch_shapes=[
-            pltpu.VMEM((4, tile // 32, 32, depth), bf16),
+            pltpu.VMEM((2, tile // 16, 16, depth), bf16),
+            pltpu.VMEM((2, tile // 16, 16, depth), bf16),
             pltpu.VMEM((per_tile, per_tile, BLK, BLK), bf16),
             pltpu.VMEM((half, per_tile, BLK, BLK), bf16),
             pltpu.VMEM((half, per_tile, BLK, BLK), bf16),
-            pltpu.VMEM((half, BLK, tile), f32),
             pltpu.VMEM((half, BLK, tile), bf16),
             pltpu.VMEM((local_rows, depth), bf16),
             pltpu.VMEM((depth, depth), bf16),
             pltpu.VMEM(block_map.shape, jnp.int32),
             pltpu.SMEM(block_map.shape, jnp.int32),
             dma((3 + per_tile,)), dma, dma((2,)), dma, dma((half,)), dma((half,)),
-            dma((2, 8)), dma((2, 8, 2)), dma((2, 7)), dma((2, 8, 2)), dma((2, 8)),
+            dma((2, 8)), dma((2, 8, 4)), dma((2, 7)), dma((2, 8, 4)), dma((2, 8)),
         ],
         compiler_params=pltpu.CompilerParams(
             collective_id=0, has_side_effects=True, vmem_limit_bytes=56 * 2**20

time: 79 us -> 74.3 us (0.941)
  Pallas kernels: 75.4 us -> 70 us
    pallas_call x1, Pallas kernels: 75.4 us -> 70 us  [shards(): pl.pallas_call(kernel, out_shape=(jax.ShapeDtypeStruct((local_rows, depth...]
where the time goes in v3:
time: 74.3 us; the launch traced here: 73.5 us
  Pallas kernels  70 us (94%)
  local copies, waits for them, and re-layouts  2.87 us (4%)
    pallas_call x1, Pallas kernels, shards(): pl.pallas_call(kernel, out_shape=(jax.ShapeDtypeStruct((local_rows, depth...  70 us
    unnamed x4, local copies, waits for them, and re-layouts  2.87 us

profile of v3, /device:TPU:41, one launch (start us, length us, event | category | flops | bytes accessed | tf_op | source)
XLA Modules:
  0.0 73.5 jit_solution(3840231088258960045)
XLA Ops:
  0.6 70.0 %panel_and_extend_add.1 = (bf16[192,512]{1,0:T(8,128)(2,1)}, f32[3,256,1536]{2,1,0:T(8,128)S(1)}) custom-call(s32[1,48]{1,0:T(1,128)} %map_any.1, s32[1,48]{1,0:T(1,128)} %fill_ref.1, s32[1,48]{1,0:T(1,128)} %map_any.1, bf16[192,512]{1,0:T(8,128)(2,1)} %bitcast.11, bf16[512,512]{1,0:T(8,128)(2,1)} %bitcast.9, bf16[6,256,1536]{2,1,0:T(8,128)(2,1)} %bitcast.7, ...), custom_call_target="tpu_custom_call" | custom-call | tf_op jit(solution)/shard_map/panel_and_extend_add/pallas_call | solution.py:302
  70.7 0.0 copy-start
  70.7 2.2 %copy.10 = f32[1,768,1536]{2,1,0:T(8,128)} copy(f32[1,768,1536]{2,1,0:T(8,128)S(1)} %bitcast.6) | data formatting | bytes 9437184
  72.9 0.0 copy-done
  72.9 0.7 copy.11
Async XLA Ops:
  70.7 2.2 %copy-start = (bf16[192,512]{1,0:T(8,128)(2,1)S(1)}, bf16[192,512]{1,0:T(8,128)(2,1)}, u32[]{:S(2)}) copy-start(bf16[192,512]{1,0:T(8,128)(2,1)} %get-tuple-element.4) | copy-start | bytes 589828

commit v4 on v3

--- a/solution.py
+++ b/solution.py
@@ -178,14 +178,16 @@
             pl.when(is_source)(lambda: arrived(e, 0, j))
         feed(e, j, near)
 
-    def pass_chain(e, dy):
+    def pass_chain(e, dy, among=None):
+        here_on = chained if among is None else jnp.logical_and(chained, among)
+        then_on = jnp.logical_and(here_on, distance < 3)
         j = ((y + dy) % 4) * 2 + core
         for h in range(parts):
             here = part(2 + e, j, h)
-            pl.when(chained)(pltpu.make_async_copy(here, here, col_recv.at[e, j, h]).wait)
-            remote(onward, here, here, chain_send.at[e, j, h], col_recv.at[e, j, h], device(zh_=next_zh))
+            pl.when(here_on)(pltpu.make_async_copy(here, here, col_recv.at[e, j, h]).wait)
+            remote(then_on, here, here, chain_send.at[e, j, h], col_recv.at[e, j, h], device(zh_=next_zh))
         here = slot(2 + e, j)
-        remote(chained, here, here, twin_send.at[e, j], col_recv.at[e, j, 0], device(core_=1 - core))
+        remote(here_on, here, here, twin_send.at[e, j], col_recv.at[e, j, 0], device(core_=1 - core))
 
     tell = pltpu.make_async_remote_copy(
         src_ref=map_any, dst_ref=far_v, send_sem=map_sems.at[0], recv_sem=map_sems.at[1],
@@ -215,19 +217,25 @@
     own(1)
     relay(0, False)
     feed_from(0, 3, False)
-    pass_chain(0, 0)
+    close = distance == 1
+    apart = distance > 1
+    pass_chain(0, 0, close)
     feed_from(0, 1, True)
     feed_from(0, 1, False)
     cross(1)
+    pass_chain(0, 0, apart)
     feed_from(0, 2, True)
-    pass_chain(0, 3)
+    pass_chain(0, 3, close)
     feed_from(0, 2, False)
     relay(1, True)
+    pass_chain(0, 3, apart)
     feed_from(1, 0, True)
-    pass_chain(0, 1)
+    pass_chain(0, 1, close)
     feed_from(1, 0, False)
-    pass_chain(0, 2)
+    pass_chain(0, 2, close)
     relay(1, False)
+    pass_chain(0, 1, apart)
+    pass_chain(0, 2, apart)
     for dy in (3, 1, 2):
         feed_from(1, dy, True)
         feed_from(1, dy, False)

time: 74.3 us -> 74.4 us (level)
  no operation moved by 1% of the time
where the time goes in v4:
time: 74.4 us; the launch traced here: 73.7 us
  Pallas kernels  70.1 us (94%)
  local copies, waits for them, and re-layouts  2.87 us (4%)
    pallas_call x1, Pallas kernels, shards(): pl.pallas_call(kernel, out_shape=(jax.ShapeDtypeStruct((local_rows, depth...  70.1 us
    unnamed x4, local copies, waits for them, and re-layouts  2.87 us

profile of v4, /device:TPU:41, one launch (start us, length us, event | category | flops | bytes accessed | tf_op | source)
XLA Modules:
  0.0 73.7 jit_solution(12270354421579030319)
XLA Ops:
  0.6 70.1 %panel_and_extend_add.1 = (bf16[192,512]{1,0:T(8,128)(2,1)}, f32[3,256,1536]{2,1,0:T(8,128)S(1)}) custom-call(s32[1,48]{1,0:T(1,128)} %map_any.1, s32[1,48]{1,0:T(1,128)} %fill_ref.1, s32[1,48]{1,0:T(1,128)} %map_any.1, bf16[192,512]{1,0:T(8,128)(2,1)} %bitcast.11, bf16[512,512]{1,0:T(8,128)(2,1)} %bitcast.9, bf16[6,256,1536]{2,1,0:T(8,128)(2,1)} %bitcast.7, ...), custom_call_target="tpu_custom_call" | custom-call | tf_op jit(solution)/shard_map/panel_and_extend_add/pallas_call | solution.py:310
  70.8 0.0 copy-start
  70.8 2.2 %copy.10 = f32[1,768,1536]{2,1,0:T(8,128)} copy(f32[1,768,1536]{2,1,0:T(8,128)S(1)} %bitcast.6) | data formatting | bytes 9437184
  73.0 0.0 copy-done
  73.0 0.7 copy.11
Async XLA Ops:
  70.8 2.2 %copy-start = (bf16[192,512]{1,0:T(8,128)(2,1)S(1)}, bf16[192,512]{1,0:T(8,128)(2,1)}, u32[]{:S(2)}) copy-start(bf16[192,512]{1,0:T(8,128)(2,1)} %get-tuple-element.4) | copy-start | bytes 589828
